TPU v7x, 512 devices: a whole 4x4x16 slice. The times are simulated.
512 devices in a mesh: docs: 64 (over x, z_lo, core), blk: 8 (over y, z_hi).
Axes of the slice: x: 4, y: 4, z: 16 (z_hi: 2, z_lo: 8; z = z_hi * 8 + z_lo), core: 2. Of those that a mesh axis runs over, the one named last changes fastest.
Arguments:
- group_rows: bfloat16 [8, 16384, 2048], P('blk', 'docs'), may hold values from -0.14941406 to 0.14941406
- group_owner: int32 [8, 16384, 1], P('blk', 'docs'), may hold values from 0 to 63; in each aligned block of 256 rows (0 to 255, 256 to 511, ..., all dimensions but the last counted through in order) at most 8 rows name the same one
- group_doc: int32 [8, 16384], P('blk', 'docs'), may hold values from 0 to 255
- doc_weight: float32 [8, 16384], P('blk', 'docs'), may hold values from 0.1 to 1
- queries: bfloat16 [256, 2048], P('blk'), may hold values from -6 to 6
- precond: bfloat16 [2048, 2048], P(None, 'docs'), may hold values from -0.125 to 0.125
Outputs:
- scores: float32 [256, 8, 16384], P(None, 'blk', 'docs')
Inputs may be any that keep to these rules, and one draw needn't show every extreme that they name: `group_owner`: within the rows of one device, at most 8 groups name the same owner, and some owner gets exactly 8.
All inputs are finite; a program needn't handle non-finite values.
Results may differ from a plain program's by a relative error of at most 0.006.
Values may be sent and summed in bfloat16 or wider, within the bound.
A program may use at most 64 MiB of HBM per device.

v0:
```python
import jax
import jax.numpy as jnp
from jax import lax
from jax.sharding import PartitionSpec as P

NT = (((1,), (1,)), ((), ()))


def shards(group_rows, group_owner, group_doc, doc_weight, queries, precond):
    rows = group_rows[0]
    owner = group_owner[0, :, 0]
    doc_index = group_doc[0]
    peers = lax.axis_size("docs")
    count = rows.shape[0]
    capacity = 2 * count // peers
    slots = peers * capacity
    peer_ids = jnp.arange(peers, dtype=jnp.int32)
    owner_table = peer_ids[:, None] == owner[None, :]
    order = jnp.arange(count, dtype=jnp.int32)
    before = (order[:, None] < order[None, :]).astype(jnp.bfloat16)
    earlier = jnp.dot(owner_table.astype(jnp.bfloat16), before, preferred_element_type=jnp.float32)
    rank = jnp.sum(jnp.where(owner_table, earlier, 0.0), axis=0).astype(jnp.int32)
    slot = owner * capacity + rank
    pick = jnp.arange(slots, dtype=jnp.int32)[:, None] == slot[None, :]
    send_ids = jnp.max(jnp.where(pick, doc_index[None, :], -1), axis=1).reshape(peers, capacity)
    got_ids = lax.all_to_all(send_ids, "docs", split_axis=0, concat_axis=0, tiled=True).reshape(
        slots
    )
    query_pre = jnp.dot(queries, precond, preferred_element_type=jnp.float32).astype(jnp.bfloat16)
    full_rows = lax.all_gather(query_pre, "docs", axis=1, tiled=True)
    full = lax.all_gather(full_rows, "blk", axis=0, tiled=True)
    part = lax.dot_general(rows, full, NT, preferred_element_type=jnp.float32).astype(jnp.bfloat16)
    send = jnp.dot(pick.astype(jnp.bfloat16), part, preferred_element_type=jnp.float32).astype(
        jnp.bfloat16
    )
    send = send.reshape(peers, capacity, send.shape[1])
    got = lax.all_to_all(send, "docs", split_axis=0, concat_axis=0, tiled=True)
    got = got.reshape(slots, got.shape[2])
    doc_ids = jnp.arange(doc_weight.shape[1], dtype=jnp.int32)
    member = (got_ids[:, None] == doc_ids[None, :]).astype(jnp.bfloat16)
    scores = lax.dot_general(
        got, member, (((0,), (0,)), ((), ())), preferred_element_type=jnp.float32
    )
    return (scores * doc_weight[0][None, :])[:, None, :]


def solution(mesh):
    return jax.shard_map(
        shards,
        mesh=mesh,
        in_specs=(
            P("blk", "docs", None),
            P("blk", "docs", None),
            P("blk", "docs"),
            P("blk", "docs"),
            P("blk", None),
            P(None, "docs"),
        ),
        out_specs=P(None, "blk", "docs"),
        check_vma=False,
    )
```

profile of v0, /device:TPU:1, one launch (start us, length us, event | category | flops | bytes accessed | tf_op | source)
XLA Modules:
  0.0 259.1 jit_solution(14440110676353129902)
XLA Ops:
  6.5 0.0 copy-start
  6.5 0.0 all-gather.2.cloned.1.call-start
  6.5 1.2 convolution_convert_fusion.2
  7.7 0.1 copy.16
  7.8 129.0 %all_gather.6 = bf16[32,2048]{0,1:T(8,128)(2,1)S(1)} all-gather(bf16[32,32]{0,1:T(8,128)(2,1)S(1)} %copy.16), channel_id=1, replica_groups=mesh['docs'=64,'blk'=8] {'docs'}, dimensions={1}, use_global_device_ids=true | all-gather | bytes 133120 | tf_op jit(solution)/shard_map/all_gather | solution.py:30
  136.8 0.8 copy.17
  137.6 0.0 all-gather.2.cloned.1.call-update
  137.7 0.0 copy-start.1
  137.7 0.7 copy-done.1
  138.4 0.2 fusion.2
  138.5 0.0 copy-start.2
  138.6 0.7 copy-done.2
  139.2 0.1 select_reduce_fusion
  139.4 0.7 all_to_all.10
  140.1 4.2 %all-to-all-start.1 = ((s32[64,1,8]{2,1,0:T(1,128)}), s32[64,1,8]{2,1,0:T(1,128)S(1)}, u32[]{:S(2)}, u32[]{:S(2)}) async-start(s32[64,1,8]{2,1,0:T(1,128)} %bitcast.5), calls=%async_computation.1 | async-start | bytes 65536 | tf_op jit(solution)/shard_map/all_to_all | solution.py:26
  144.3 77.4 %all-gather.2.cloned.1.call-done = bf16[256,2048]{1,0:T(8,128)(2,1)} async-done(((bf16[32,2048]{1,0:T(8,128)(2,1)}), bf16[256,2048]{1,0:T(8,128)(2,1)}) %all-gather.2.cloned.1.call-update) | async-done | bytes 1048592 | tf_op jit(solution)/shard_map/all_gather | solution.py:31
  221.7 0.0 copy-done
  221.7 2.7 %fusion.1 = bf16[64,8,256]{2,1,0:T(8,128)(2,1)} fusion(bf16[256,2048]{1,0:T(8,128)(2,1)} %all-gather.2.cloned.1.call-done, bf16[1,256,2048]{2,1,0:T(8,128)(2,1)S(1)} %copy-done, s32[256]{0:T(256)S(1)} %convert_add_fusion), kind=kOutput, calls=%fused_computation.3 | convolution fusion | flops 335872000 | bytes 2360320 | tf_op jit(solution)/shard_map/dot_general | solution.py:33
  224.4 0.0 all-to-all-done.1
  224.4 7.2 %all-to-all-start = ((bf16[64,8,256]{2,1,0:T(8,128)(2,1)}), bf16[64,8,256]{2,1,0:T(8,128)(2,1)S(1)}, u32[]{:S(2)}, u32[]{:S(2)}) async-start(bf16[64,8,256]{2,1,0:T(8,128)(2,1)} %fusion.1), calls=%async_computation | async-start | bytes 524288 | tf_op jit(solution)/shard_map/all_to_all | solution.py:37
  231.6 0.6 broadcast.7
  232.2 0.7 reduce.3
  232.9 0.1 eq.47
  233.0 0.0 copy-start.3
  233.0 17.9 %all-to-all-done = bf16[64,8,256]{2,1,0:T(8,128)(2,1)S(1)} async-done(((bf16[64,8,256]{2,1,0:T(8,128)(2,1)}), bf16[64,8,256]{2,1,0:T(8,128)(2,1)S(1)}, u32[]{:S(2)}, u32[]{:S(2)}) %all-to-all-start) | async-done | bytes 262176 | tf_op jit(solution)/shard_map/all_to_all | solution.py:37
  250.9 0.0 copy-done.3
  250.9 0.3 fusion
  251.2 1.0 copy.19
  (1 shorter events, 0.0 us)
Async XLA Ops:
  6.5 215.1 %copy-start = (bf16[1,256,2048]{2,1,0:T(8,128)(2,1)S(1)}, bf16[1,256,2048]{2,1,0:T(8,128)(2,1)}, u32[]{:S(2)}) copy-start(bf16[1,256,2048]{2,1,0:T(8,128)(2,1)} %param.6) | copy-start | bytes 3145732
  6.5 215.1 %all-gather.2.cloned.1.call-start = ((), (), s32[]{:S(2)}) async-start(), calls=%async_computation.2 | async-start | bytes 1179648 | tf_op jit(solution)/shard_map/all_gather | solution.py:31
  137.7 0.7 copy-start.1
  138.5 0.7 copy-start.2
  140.1 84.3 %all-to-all-start.1 = ((s32[64,1,8]{2,1,0:T(1,128)}), s32[64,1,8]{2,1,0:T(1,128)S(1)}, u32[]{:S(2)}, u32[]{:S(2)}) async-start(s32[64,1,8]{2,1,0:T(1,128)} %bitcast.5), calls=%async_computation.1 | async-start | bytes 65536 | tf_op jit(solution)/shard_map/all_to_all | solution.py:26
  224.4 26.5 %all-to-all-start = ((bf16[64,8,256]{2,1,0:T(8,128)(2,1)}), bf16[64,8,256]{2,1,0:T(8,128)(2,1)S(1)}, u32[]{:S(2)}, u32[]{:S(2)}) async-start(bf16[64,8,256]{2,1,0:T(8,128)(2,1)} %fusion.1), calls=%async_computation | async-start | bytes 524288 | tf_op jit(solution)/shard_map/all_to_all | solution.py:37
  233.0 17.9 %copy-start.3 = (f32[1,256]{1,0:T(1,128)S(1)}, f32[1,256]{1,0:T(1,128)}, u32[]{:S(2)}) copy-start(f32[1,256]{1,0:T(1,128)} %param.9) | copy-start | bytes 3076
Sparse Core Ops, SparseCore 0:
  137.8 83.8 all-gather.1
where the time goes:
time: 259 us
  blocking collectives  129 us (50%)
  waiting for transfers between devices  95.3 us (37%)
  between operations  13.5 us (5%)
  starting transfers between devices  11.4 us (4%)
  local copies, waits for them, and re-layouts  4.65 us (2%)
  matrix products  4.45 us (2%)
    all_gather x1, blocking collectives, shards(): full_rows = lax.all_gather(query_pre, 'docs', axis=1, tiled=True)  129 us
    all_gather x1, waiting for transfers between devices, shards(): full = lax.all_gather(full_rows, 'blk', axis=0, tiled=True)  77.4 us
    all_to_all x1, waiting for transfers between devices, shards(): got = lax.all_to_all(send, 'docs', split_axis=0, concat_axis=0, tiled=True)  17.9 us
    all_to_all x1, starting transfers between devices, shards(): got = lax.all_to_all(send, 'docs', split_axis=0, concat_axis=0, tiled=True)  7.2 us
  transfers between devices with their start and end apart: 3, of which 2 were waited for; matrix products, arithmetic and copies ran while one was open for 2% of the time, Pallas kernels for 0%

commit v1 on v0

--- a/solution.py
+++ b/solution.py
@@ -27,7 +27,9 @@
         slots
     )
     query_pre = jnp.dot(queries, precond, preferred_element_type=jnp.float32).astype(jnp.bfloat16)
-    full_rows = lax.all_gather(query_pre, "docs", axis=1, tiled=True)
+    full_rows = jnp.concatenate(
+        lax.all_to_all(jnp.stack([query_pre] * lax.axis_size("docs")), "docs", 0, 0), axis=1
+    )
     full = lax.all_gather(full_rows, "blk", axis=0, tiled=True)
     part = lax.dot_general(rows, full, NT, preferred_element_type=jnp.float32).astype(jnp.bfloat16)
     send = jnp.dot(pick.astype(jnp.bfloat16), part, preferred_element_type=jnp.float32).astype(

time: 259 us -> 164 us (0.63)
  blocking collectives: 129 us -> 31.4 us
    all_gather x1 -> x0, blocking collectives: 129 us -> none  [shards(): full_rows = lax.all_gather(query_pre, 'docs', axis=1, tiled=True)]
    all_to_all x0 -> x1, blocking collectives: none -> 31.4 us  [shards(): lax.all_to_all(jnp.stack([query_pre] * lax.axis_size('docs')), 'docs', 0, 0)]
  transfers between devices with their start and end apart: 3 -> 3, of which waited for: 2 -> 2; matrix products, arithmetic and copies ran while one was open for 2% -> 3% of each run, Pallas kernels for 0% -> 0%
where the time goes in v1:
time: 164 us
  waiting for transfers between devices  94.1 us (57%)
  blocking collectives  31.4 us (19%)
  between operations  13.5 us (8%)
  starting transfers between devices  13.3 us (8%)
  local copies, waits for them, and re-layouts  5.89 us (4%)
  matrix products  4.46 us (3%)
    all_gather x1, waiting for transfers between devices, shards(): full = lax.all_gather(full_rows, 'blk', axis=0, tiled=True)  76.2 us
    all_to_all x1, blocking collectives, shards(): lax.all_to_all(jnp.stack([query_pre] * lax.axis_size('docs')), 'docs', 0, 0)  31.4 us
    all_to_all x1, waiting for transfers between devices, shards(): got = lax.all_to_all(send, 'docs', split_axis=0, concat_axis=0, tiled=True)  17.9 us
    all_to_all x1, starting transfers between devices, shards(): got = lax.all_to_all(send, 'docs', split_axis=0, concat_axis=0, tiled=True)  7.19 us
    all_to_all x1, starting transfers between devices, shards(): lax.all_to_all(send_ids, 'docs', split_axis=0, concat_axis=0, tiled=True)  6.06 us
  transfers between devices with their start and end apart: 3, of which 2 were waited for; matrix products, arithmetic and copies ran while one was open for 3% of the time, Pallas kernels for 0%

profile of v1, /device:TPU:1, one launch (start us, length us, event | category | flops | bytes accessed | tf_op | source)
XLA Modules:
  0.0 163.5 jit_solution(14101425384419733864)
XLA Ops:
  6.5 0.0 copy-start
  6.5 0.0 all-gather.2.cloned.1.call-start
  6.5 1.2 convolution_convert_fusion.2
  7.7 0.1 stack.2
  7.8 0.4 reshape.43
  8.3 31.4 %all_to_all.19 = bf16[64,2,512]{2,1,0:T(2,128)(2,1)S(1)} all-to-all(bf16[64,2,512]{2,1,0:T(2,128)(2,1)S(1)} %reshape.43), channel_id=1, replica_groups=mesh['docs'=64,'blk'=8] {'docs'}, dimensions={0} | all-to-all | bytes 262144 | tf_op jit(solution)/shard_map/all_to_all | solution.py:31
  39.7 0.3 reshape.44
  40.0 0.2 copy.12
  40.2 1.2 reshape.31
  41.4 0.0 all-gather.2.cloned.1.call-update
  41.4 0.0 copy-start.1
  41.4 0.7 copy-done.1
  42.1 0.2 fusion.2
  42.3 0.0 copy-start.2
  42.3 0.7 copy-done.2
  43.0 0.1 select_reduce_fusion
  43.1 0.7 all_to_all.14
  43.8 6.1 %all-to-all-start.2 = ((s32[64,1,8]{2,1,0:T(1,128)}), s32[64,1,8]{2,1,0:T(1,128)S(1)}, u32[]{:S(2)}, u32[]{:S(2)}) async-start(s32[64,1,8]{2,1,0:T(1,128)} %bitcast.6), calls=%async_computation.2 | async-start | bytes 65536 | tf_op jit(solution)/shard_map/all_to_all | solution.py:26
  49.9 76.2 %all-gather.2.cloned.1.call-done = bf16[256,2048]{1,0:T(8,128)(2,1)} async-done(((bf16[32,2048]{1,0:T(8,128)(2,1)}), bf16[256,2048]{1,0:T(8,128)(2,1)}) %all-gather.2.cloned.1.call-update) | async-done | bytes 1048592 | tf_op jit(solution)/shard_map/all_gather | solution.py:33
  126.1 0.0 copy-done
  126.1 2.7 %fusion.1 = bf16[64,8,256]{2,1,0:T(8,128)(2,1)} fusion(bf16[256,2048]{1,0:T(8,128)(2,1)} %all-gather.2.cloned.1.call-done, bf16[1,256,2048]{2,1,0:T(8,128)(2,1)S(1)} %copy-done, s32[256]{0:T(256)S(1)} %convert_add_fusion), kind=kOutput, calls=%fused_computation.3 | convolution fusion | flops 335872000 | bytes 2360320 | tf_op jit(solution)/shard_map/dot_general | solution.py:35
  128.8 0.0 all-to-all-done.2
  128.8 7.2 %all-to-all-start.1 = ((bf16[64,8,256]{2,1,0:T(8,128)(2,1)}), bf16[64,8,256]{2,1,0:T(8,128)(2,1)S(1)}, u32[]{:S(2)}, u32[]{:S(2)}) async-start(bf16[64,8,256]{2,1,0:T(8,128)(2,1)} %fusion.1), calls=%async_computation.1 | async-start | bytes 524288 | tf_op jit(solution)/shard_map/all_to_all | solution.py:39
  136.0 0.6 broadcast.9
  136.6 0.7 reduce.3
  137.3 0.1 eq.47
  137.4 0.0 copy-start.3
  137.4 17.9 %all-to-all-done.1 = bf16[64,8,256]{2,1,0:T(8,128)(2,1)S(1)} async-done(((bf16[64,8,256]{2,1,0:T(8,128)(2,1)}), bf16[64,8,256]{2,1,0:T(8,128)(2,1)S(1)}, u32[]{:S(2)}, u32[]{:S(2)}) %all-to-all-start.1) | async-done | bytes 262176 | tf_op jit(solution)/shard_map/all_to_all | solution.py:39
  155.3 0.0 copy-done.3
  155.3 0.3 fusion
  155.7 1.0 copy.14
  (1 shorter events, 0.0 us)
Async XLA Ops:
  6.5 119.6 %copy-start = (bf16[1,256,2048]{2,1,0:T(8,128)(2,1)S(1)}, bf16[1,256,2048]{2,1,0:T(8,128)(2,1)}, u32[]{:S(2)}) copy-start(bf16[1,256,2048]{2,1,0:T(8,128)(2,1)} %param.6) | copy-start | bytes 3145732
  6.5 119.6 %all-gather.2.cloned.1.call-start = ((), (), s32[]{:S(2)}) async-start(), calls=%async_computation.3 | async-start | bytes 1179648 | tf_op jit(solution)/shard_map/all_gather | solution.py:33
  41.4 0.7 copy-start.1
  42.3 0.7 copy-start.2
  43.8 85.0 %all-to-all-start.2 = ((s32[64,1,8]{2,1,0:T(1,128)}), s32[64,1,8]{2,1,0:T(1,128)S(1)}, u32[]{:S(2)}, u32[]{:S(2)}) async-start(s32[64,1,8]{2,1,0:T(1,128)} %bitcast.6), calls=%async_computation.2 | async-start | bytes 65536 | tf_op jit(solution)/shard_map/all_to_all | solution.py:26
  128.8 26.5 %all-to-all-start.1 = ((bf16[64,8,256]{2,1,0:T(8,128)(2,1)}), bf16[64,8,256]{2,1,0:T(8,128)(2,1)S(1)}, u32[]{:S(2)}, u32[]{:S(2)}) async-start(bf16[64,8,256]{2,1,0:T(8,128)(2,1)} %fusion.1), calls=%async_computation.1 | async-start | bytes 524288 | tf_op jit(solution)/shard_map/all_to_all | solution.py:39
  137.4 17.9 %copy-start.3 = (f32[1,256]{1,0:T(1,128)S(1)}, f32[1,256]{1,0:T(1,128)}, u32[]{:S(2)}) copy-start(f32[1,256]{1,0:T(1,128)} %param.9) | copy-start | bytes 3076
Sparse Core Ops, SparseCore 0:
  41.5 84.5 all-gather.1
